TPU v7x, 32 devices: a whole 2x2x4 slice. The times are simulated.
32 devices in a mesh: groups: 2 (over y), shard: 2 (over x), expert: 4 (over z), section: 2 (over core).
Axes of the slice: x: 2, y: 2, z: 4, core: 2. Of those that a mesh axis runs over, the one named last changes fastest.
Arguments:
- tokens: bfloat16 [2, 512, 6144], P(None, ('groups', 'shard', 'expert')), parts along dimension 1, may hold values from -6 to 6
- norm_gain: float32 [2, 6144], P('section'), may hold values from 0.5 to 2
- route_ids: int32 [2, 2, 512, 2], P('section', None, ('groups', 'shard', 'expert')), parts along dimension 2, may hold values from 0 to 3, all different within a row; in each aligned block of 32 rows (0 to 31, 32 to 63, ..., all dimensions but the last counted through in order) at most 18 rows name the same one
- route_weights: float32 [2, 2, 512, 2], P('section', None, ('groups', 'shard', 'expert')), parts along dimension 2, may hold values from 0.25 to 1
- gate_blocks: bfloat16 [2, 4, 64, 1, 128, 128], P('section', 'expert', 'shard'), may hold values from -0.5 to 0.5
- up_blocks: bfloat16 [2, 4, 64, 1, 128, 128], P('section', 'expert', 'shard'), may hold values from -0.5 to 0.5
- down_blocks: bfloat16 [2, 4, 64, 1, 128, 128], P('section', 'expert', 'shard'), may hold values from -0.4375 to 0.4375
- gate_rows: int32 [2, 4, 64, 1], P('section', 'expert', 'shard'), may hold values from 0 to 47
- down_cols: int32 [2, 4, 64, 1], P('section', 'expert', 'shard'), may hold values from 0 to 47
Outputs:
- hidden_states: bfloat16 [2, 2, 512, 6144], P('section', None, ('groups', 'shard', 'expert')), parts along dimension 2
There are 2 independent parts, one for each index of `groups`. A program takes and returns all parts, laid end to end along the dimension named above; an argument that names none is the same for every part. Nothing has to cross between parts.
Inputs may be any that keep to these rules, and one draw needn't show every extreme that they name: `route_ids`: the 2 experts of a token differ; among the 32 tokens of one device, one micro-batch and one layer, no expert is named by more than 18 tokens, a bound that some block reaches of them.
All inputs are finite; a program needn't handle non-finite values.
Results may differ from a plain program's by a relative error of at most 0.0064.
Values may be sent and summed in bfloat16 or wider, within the bound.
A program may use at most 64 MiB of HBM per device.

v0:
```python
import functools
import math

import jax
import jax.numpy as jnp
from jax import lax
from jax.experimental import pallas as pl
from jax.experimental.pallas import tpu as pltpu
from jax.sharding import PartitionSpec as P

TOP = 2
EPS = 1e-05
BF16 = jnp.bfloat16
F32 = jnp.float32


def layer_kernel(
    dims,
    tokens, gain, ids, mix, gate_hbm, up_hbm, down_hbm, rows_in, cols_in,
    out,
    held, disp, comb, meta_here, normed, wide, send, recv, parts, ret_send, ret_recv, weights, meta_v, meta_s,
    tok_sem, hand_sem, own_sem, meta_own_sem, meta_send_sem, meta_recv_sem, meta_copy_sem,
    wx_send, wx_recv, wy_send, wy_recv, disp_send, disp_recv, disp_self,
    back_send, back_recv, back_self, go_sem,
):
    micro, rows, blocks, blk, cap, experts, shards, groups, sections, n_blk = dims
    slots = experts * cap
    me_g, me_s = lax.axis_index("groups"), lax.axis_index("shard")
    me_e, me_l = lax.axis_index("expert"), lax.axis_index("section")
    sizes = {"groups": groups, "shard": shards, "expert": experts, "section": sections}
    place = {"groups": me_g, "shard": me_s, "expert": me_e, "section": me_l}
    half = n_blk // groups
    cuts = math.gcd(half, 4)
    step = half // cuts
    sources = (gate_hbm, up_hbm, down_hbm)

    def remote(src, dst, ssem, rsem, axis, index):
        return pltpu.make_async_remote_copy(
            src_ref=src, dst_ref=dst, send_sem=ssem, recv_sem=rsem,
            device_id={axis: index}, device_id_type=pl.DeviceIdType.MESH,
        )

    def peer(axis, by):
        return lax.rem(place[axis] + by, sizes[axis])

    own = [
        pltpu.make_async_copy(sources[a], weights.at[a, me_s], own_sem.at[a]) for a in range(3)
    ]
    for copy in own:
        copy.start()

    def token_copy(m):
        return pltpu.make_async_copy(tokens.at[m], held.at[m], tok_sem.at[m])

    @pl.when(me_l == 0)
    def _():
        for m in range(micro):
            token_copy(m).start()

    meta_own = pltpu.make_async_copy(meta_here, meta_v.at[me_s], meta_own_sem)

    barrier = pltpu.get_barrier_semaphore()
    for axis in ("groups", "shard", "expert", "section"):
        for by in range(1, sizes[axis]):
            pl.semaphore_signal(
                barrier, inc=1, device_id={axis: peer(axis, by)},
                device_id_type=pl.DeviceIdType.MESH,
            )

    pl.semaphore_wait(barrier, sum(n - 1 for n in sizes.values()))

    def hand_copy(m):
        return remote(
            out.at[m], held.at[m], hand_sem.at[0, m], hand_sem.at[1, m], "section",
            peer("section", 1),
        )

    def part(group, a, k, shard):
        return weights.at[a, shard, pl.ds(group * half + k * step, step)]

    def over_shard(a, k, by):
        i = k * 3 + a
        src = sources[a].at[pl.ds(me_g * half + k * step, step)]
        return remote(
            src, part(me_g, a, k, me_s), wx_send.at[i, by], wx_recv.at[i, by], "shard",
            peer("shard", by),
        )

    def over_groups(a, k, by, hop):
        i = k * 3 + a
        spot = part(me_g, a, k, peer("shard", shards - by))
        return remote(
            spot, spot, wy_send.at[i, by, hop], wy_recv.at[i, by, hop], "groups",
            peer("groups", hop),
        )

    def meta_over_shard(by):
        return remote(
            meta_here, meta_v.at[me_s], meta_send_sem.at[by], meta_recv_sem.at[by], "shard",
            peer("shard", by),
        )

    order = [(a, k, by) for k in range(cuts) for a in range(3) for by in range(1, shards)]

    def start_weights():
        for a, k, by in order:
            over_shard(a, k, by).start()

    def relay_weights(first, end):
        for a, k, by in order:
            if first <= k < end:
                over_shard(a, k, by).wait_recv()
                for hop in range(1, groups):
                    over_groups(a, k, by, hop).start()

    def finish_relay(at):
        for a, k, by in order:
            if k == at:
                for hop in range(1, groups):
                    over_groups(a, k, by, hop).wait()

    early = cuts

    def relay_in_time(first, end):
        @pl.when(me_l == 0)
        def _():
            relay_weights(first, end)

    def chunk_out(m, by):
        return remote(
            send.at[m, peer("expert", by)], recv.at[m, me_e], disp_send.at[m, by],
            disp_recv.at[m, by], "expert", peer("expert", by),
        )

    def chunk_self(m):
        return pltpu.make_async_copy(send.at[m, me_e], recv.at[m, me_e], disp_self.at[m])

    def chunk_back(m, by):
        return remote(
            ret_send.at[m, peer("expert", by)], ret_recv.at[m, me_e], back_send.at[m, by],
            back_recv.at[m, by], "expert", peer("expert", by),
        )

    def back_own(m):
        return pltpu.make_async_copy(ret_send.at[m, me_e], ret_recv.at[m, me_e], back_self.at[m])

    far_first = sorted(range(1, experts), key=lambda by: abs(by - experts // 2))

    def lanes(r):
        return pl.ds(pl.multiple_of(r * blk, blk), blk)

    def chunk_rows(e):
        return pl.ds(pl.multiple_of(e * (cap * blocks), 16), cap * blocks)

    def strided(r):
        return pl.ds(r, slots, stride=blocks)

    def dispatch(m):
        values = held[m].astype(F32)
        scale = lax.rsqrt(jnp.mean(values * values, axis=-1, keepdims=True) + EPS)
        normed[...] = (values * scale * gain[...]).astype(BF16)

        @pl.loop(0, blocks, unroll=8)
        def _(r):
            wide[strided(r), :] = jnp.dot(
                disp[m], normed[:, lanes(r)], preferred_element_type=F32
            )

        for by in far_first + [0]:
            e = peer("expert", by)
            send[m, e] = wide[chunk_rows(e), :].astype(BF16)
            if by > 0:
                chunk_out(m, by).start()
        chunk_self(m).start()

    def segment(s, k):
        products = []
        for group in range(groups):
            for u in range(step):
                c = group * half + k * step + u
                at = (k * groups + group) * step + u
                x = wide[strided(meta_s[s, 0, c]), :].astype(BF16)
                gate = jnp.dot(x, weights[0, s, c], preferred_element_type=F32)
                up = jnp.dot(x, weights[1, s, c], preferred_element_type=F32)
                hidden = (gate / (1.0 + jnp.exp(-gate)) * up).astype(BF16)
                product = jnp.dot(hidden, weights[2, s, c], preferred_element_type=F32)
                products.append((at, c, product))
        for at, c, product in products:
            parts[s, at] = product + parts[s, meta_s[s, 1, c]]

    def expert_part(m, first):
        chunk_self(m).wait()
        wide[chunk_rows(me_e), :] = recv[m, me_e].astype(F32)
        for by in far_first:
            chunk_out(m, by).wait()
            e = peer("expert", experts - by)
            wide[chunk_rows(e), :] = recv[m, e].astype(F32)
        if first:
            for copy in own:
                copy.wait()
            for by in range(1, shards):
                meta_over_shard(by).wait()
            meta_own.wait()
            load = pltpu.make_async_copy(meta_v, meta_s, meta_copy_sem)
            load.start()
            load.wait()

            @pl.loop(0, cuts)
            def _(k):
                segment(me_s, k)

            for k in range(cuts):
                if k == 0:
                    relay_in_time(early, min(early + 1, cuts))
                elif early + k < cuts:
                    relay_in_time(early + k, early + k + 1)
                finish_relay(k)

                @pl.loop(1, shards)
                def _(by):
                    segment(peer("shard", shards - by), k)

                if k == max(0, cuts - early - 1):
                    @pl.when((me_l == 0) & (me_l < sections - 1))
                    def _():
                        pl.semaphore_signal(
                            go_sem, inc=1, device_id={"section": peer("section", 1)},
                            device_id_type=pl.DeviceIdType.MESH,
                        )
            for a, k, by in order:
                over_shard(a, k, by).wait_send()
        else:
            @pl.loop(0, shards)
            def _(s):
                @pl.loop(0, cuts)
                def _(k):
                    segment(s, k)

        @pl.loop(0, blocks, unroll=4)
        def _(j):
            total = parts[0, meta_s[0, 2, j]]
            for s in range(1, shards):
                total = total + parts[s, meta_s[s, 2, j]]
            wide[strided(j), :] = total

        for by in far_first + [0]:
            e = peer("expert", by)
            ret_send[m, e] = wide[chunk_rows(e), :].astype(BF16)
            if by > 0:
                chunk_back(m, by).start()
        back_own(m).start()

    def combine(m):
        back_own(m).wait()
        wide[chunk_rows(me_e), :] = ret_recv[m, me_e].astype(F32)
        for by in far_first:
            chunk_back(m, by).wait()
            e = peer("expert", experts - by)
            wide[chunk_rows(e), :] = ret_recv[m, e].astype(F32)

        @pl.loop(0, blocks, unroll=8)
        def _(r):
            mixed = jnp.dot(
                comb[m], wide[strided(r), :], preferred_element_type=F32,
                precision=lax.Precision.HIGHEST,
            )
            out[m, :, lanes(r)] = (held[m, :, lanes(r)].astype(F32) + mixed).astype(BF16)

    @pl.when(me_l == 0)
    def _():
        start_weights()

    def arrival(c):
        group = sum((c >= g * half).astype(jnp.int32) for g in range(1, groups))
        within = c - group * half
        k = sum((within >= i * step).astype(jnp.int32) for i in range(1, cuts))
        return k * (groups - 1) * step + group * step + within

    def iota(shape, axis):
        return lax.broadcasted_iota(jnp.int32, shape, axis)

    cols = cols_in[...]
    cols_down = jnp.transpose(jnp.broadcast_to(cols, (n_blk, n_blk)))
    from_place = arrival(iota((n_blk, n_blk), 0))
    chained = (cols_down == cols) & (from_place < arrival(iota((n_blk, n_blk), 1)))
    before = jnp.max(jnp.where(chained, from_place, -1), axis=0, keepdims=True)
    final = jnp.broadcast_to(cols_down[:, :1], (n_blk, blocks)) == iota((n_blk, blocks), 1)
    last = jnp.where(final, arrival(iota((n_blk, blocks), 0)), -1)
    last = jnp.max(last, axis=0, keepdims=True)
    meta_here[...] = jnp.zeros_like(meta_here)
    meta_here[0:1, 0:n_blk] = rows_in[...]
    meta_here[1:2, 0:n_blk] = jnp.where(before < 0, n_blk, before)
    meta_here[2:3, 0:blocks] = jnp.where(last < 0, n_blk, last)

    slot = iota((slots, rows), 0)
    expert = sum((slot >= e * cap).astype(jnp.int32) for e in range(1, experts))
    place_in = (slot - expert * cap).astype(F32)
    earlier = (iota((rows, rows), 0) < iota((rows, rows), 1)).astype(F32).astype(BF16)
    for m in range(micro):
        named = [ids[m, j:j + 1, :] == expert for j in range(TOP)]
        hit = functools.reduce(jnp.logical_or, named)
        ahead = jnp.dot(
            hit.astype(F32).astype(BF16), earlier, preferred_element_type=F32
        )
        fits = hit & (ahead == place_in)
        amount = sum(jnp.where(named[j], mix[m, j:j + 1, :], 0.0) for j in range(TOP))
        disp[m] = fits.astype(F32).astype(BF16)
        comb[m] = jnp.transpose(jnp.where(fits, amount, 0.0))

    meta_own.start()
    for by in range(1, shards):
        meta_over_shard(by).start()
    for s in range(shards):
        parts[s, n_blk] = jnp.zeros_like(parts[s, n_blk])

    @pl.when(me_l == 0)
    def _():
        for m in range(micro):
            token_copy(m).wait()
            dispatch(m)
        relay_weights(0, early)

    @pl.when(me_l > 0)
    def _():
        pl.semaphore_wait(go_sem, 1)
        start_weights()
        relay_weights(0, cuts)

    @pl.when((me_l > 0) & (me_l < sections - 1))
    def _():
        pl.semaphore_signal(
            go_sem, inc=1, device_id={"section": peer("section", 1)},
            device_id_type=pl.DeviceIdType.MESH,
        )

    @pl.when(me_l > 0)
    def _():
        for m in range(micro):
            hand_copy(m).wait_recv()
            dispatch(m)

    for m in range(micro):
        expert_part(m, m == 0)
    for m in range(micro):
        combine(m)

        @pl.when(me_l < sections - 1)
        def _():
            hand_copy(m).start()

    @pl.when(me_l < sections - 1)
    def _():
        for m in range(micro):
            hand_copy(m).wait_send()


def body(
    sizes,
    tokens,
    norm_gain,
    route_ids,
    route_weights,
    gate_blocks,
    up_blocks,
    down_blocks,
    gate_rows,
    down_cols,
):
    groups, shards, experts, sections = sizes
    micro, rows, width = tokens.shape
    n_blk, blk = gate_blocks.shape[2], gate_blocks.shape[-1]
    blocks = width // blk
    cap = min(rows, max(rows * 9 // 16, rows * TOP // experts + 2))
    slots = experts * cap

    cuts = math.gcd(n_blk // groups, 4)
    meta_width = -(-max(n_blk, blocks) // 128) * 128
    pieces = 3 * cuts
    dims = (micro, rows, blocks, blk, cap, experts, shards, groups, sections, n_blk)
    dma = pltpu.SemaphoreType.DMA
    chunk = (micro, experts, cap * blocks, blk)
    vmem, anywhere = pl.BlockSpec(memory_space=pltpu.VMEM), pl.BlockSpec(memory_space=pl.ANY)
    out = pl.pallas_call(
        functools.partial(layer_kernel, dims),
        out_shape=jax.ShapeDtypeStruct((micro, rows, width), BF16),
        in_specs=[anywhere] + [vmem] * 3 + [anywhere] * 3 + [vmem] * 2,
        out_specs=vmem,
        scratch_shapes=[
            pltpu.VMEM((micro, rows, width), BF16),
            pltpu.VMEM((micro, slots, rows), BF16),
            pltpu.VMEM((micro, rows, slots), F32),
            pltpu.VMEM((8, meta_width), jnp.int32),
            pltpu.VMEM((rows, width), BF16),
            pltpu.VMEM((slots * blocks, blk), F32),
            pltpu.VMEM(chunk, BF16),
            pltpu.VMEM(chunk, BF16),
            pltpu.VMEM((shards, n_blk + 1, slots, blk), F32),
            pltpu.VMEM(chunk, BF16),
            pltpu.VMEM(chunk, BF16),
            pltpu.VMEM((3, shards, n_blk, blk, blk), BF16),
            pltpu.VMEM((shards, 8, meta_width), jnp.int32),
            pltpu.SMEM((shards, 8, meta_width), jnp.int32),
            dma((micro,)),
            dma((2, micro)),
            dma((3,)),
            dma,
            dma((shards,)),
            dma((shards,)),
            dma,
            dma((pieces, shards)),
            dma((pieces, shards)),
            dma((pieces, shards, groups)),
            dma((pieces, shards, groups)),
            dma((micro, experts)),
            dma((micro, experts)),
            dma((micro,)),
            dma((micro, experts)),
            dma((micro, experts)),
            dma((micro,)),
            pltpu.SemaphoreType.REGULAR,
        ],
        compiler_params=pltpu.CompilerParams(
            collective_id=0, has_side_effects=True, vmem_limit_bytes=56 * 1024 * 1024
        ),
    )(
        tokens, norm_gain, jnp.swapaxes(route_ids[0], 1, 2), jnp.swapaxes(route_weights[0], 1, 2),
        gate_blocks.reshape(n_blk, blk, blk), up_blocks.reshape(n_blk, blk, blk),
        down_blocks.reshape(n_blk, blk, blk), gate_rows.reshape(1, n_blk),
        down_cols.reshape(1, n_blk),
    )
    return out[None]


def solution(mesh):
    sizes = tuple(mesh.shape[name] for name in ("groups", "shard", "expert", "section"))
    in_specs = (
        P(None, ("groups", "shard", "expert"), None),
        P("section", None),
        P("section", None, ("groups", "shard", "expert"), None),
        P("section", None, ("groups", "shard", "expert"), None),
        P("section", "expert", "shard", None, None, None),
        P("section", "expert", "shard", None, None, None),
        P("section", "expert", "shard", None, None, None),
        P("section", "expert", "shard", None),
        P("section", "expert", "shard", None),
    )
    out_specs = P("section", None, ("groups", "shard", "expert"), None)
    return jax.shard_map(
        functools.partial(body, sizes), mesh=mesh, in_specs=in_specs, out_specs=out_specs,
        check_vma=False,
    )
```

profile of v0, /device:TPU:9, one launch (start us, length us, event | category | flops | bytes accessed | tf_op | source)
XLA Modules:
  0.0 95.5 jit_solution(9269899588592380418)
XLA Ops:
  0.0 93.4 %shard_map.91 = bf16[2,32,6144]{2,1,0:T(8,128)(2,1)} custom-call(bf16[2,32,6144]{2,1,0:T(8,128)(2,1)} %tokens.1, f32[1,6144]{1,0:T(1,128)} %gain.1, s32[2,2,32]{2,1,0:T(2,128)} %bitcast.16, f32[2,2,32]{2,1,0:T(2,128)} %bitcast.17, bf16[32,128,128]{2,1,0:T(8,128)(2,1)} %bitcast.13, bf16[32,128,128]{2,1,0:T(8,128)(2,1)} %bitcast.14, ...), custom_call_target="tpu_custom_call" | custom-call | tf_op jit(solution)/shard_map/pallas_call | solution.py:383
  93.5 2.1 %copy.11 = bf16[1,2,32,6144]{3,2,1,0:T(8,128)(2,1)} copy(bf16[1,2,32,6144]{3,2,1,0:T(8,128)(2,1)} %bitcast.12) | data formatting | bytes 1572864
where the time goes:
time: 96.3 us; the launch traced here: 95.5 us
  Pallas kernels  93.4 us (97%)
  local copies, waits for them, and re-layouts  2.06 us (2%)
    pallas_call x1, Pallas kernels, body(): pl.pallas_call(functools.partial(layer_kernel, dims), out_shape=jax.Shape...  93.4 us
    unnamed x1, local copies, waits for them, and re-layouts  2.06 us

commit v1 on v0

v1 whole, which is shorter than its diff:
```python
import functools
import math

import jax
import jax.numpy as jnp
from jax import lax
from jax.experimental import pallas as pl
from jax.experimental.pallas import tpu as pltpu
from jax.sharding import PartitionSpec as P

TOP = 2
EPS = 1e-05
BF16 = jnp.bfloat16
F32 = jnp.float32
CUTS = 8


def layer_kernel(
    dims,
    tokens, gain, ids, mix, gate_hbm, up_hbm, down_hbm, rows_in, cols_in,
    out,
    held, disp, comb, comb_in, pieces, meta_here, normed, tails, send, recv, parts, ret_send, ret_recv,
    weights, meta_v, meta_s,
    tok_sem, hand_sem, own_sem, meta_own_sem, meta_send_sem, meta_recv_sem, meta_copy_sem, comb_sem,
    wx_send, wx_recv, wy_send, wy_recv, disp_send, disp_recv, disp_self,
    back_send, back_recv, back_self, go_sem,
):
    micro, rows, blocks, blk, cap, experts, shards, groups, sections, n_blk = dims
    main = cap // 16 * 16
    tail = cap - main
    tails_all = -(-(experts * tail) // 8) * 8
    slots = experts * main + tails_all
    folds = blocks // main
    tails_by = tails.reshape(blocks, tails_all, blk)
    me_g, me_s = lax.axis_index("groups"), lax.axis_index("shard")
    me_e, me_l = lax.axis_index("expert"), lax.axis_index("section")
    sizes = {"groups": groups, "shard": shards, "expert": experts, "section": sections}
    place = {"groups": me_g, "shard": me_s, "expert": me_e, "section": me_l}
    half = n_blk // groups
    cuts = math.gcd(half, CUTS)
    step = half // cuts
    sources = (gate_hbm, up_hbm, down_hbm)
    first, last = me_l == 0, me_l == sections - 1

    def remote(src, dst, ssem, rsem, device):
        return pltpu.make_async_remote_copy(
            src_ref=src, dst_ref=dst, send_sem=ssem, recv_sem=rsem,
            device_id=device, device_id_type=pl.DeviceIdType.MESH,
        )

    def peer(axis, by):
        return lax.rem(place[axis] + by, sizes[axis])

    def signal(sem, device):
        pl.semaphore_signal(sem, inc=1, device_id=device, device_id_type=pl.DeviceIdType.MESH)

    barrier = pltpu.get_barrier_semaphore()
    for by in range(experts - 1, 0, -1):
        signal(barrier, {"expert": peer("expert", by)})
        for hop in range(1, sections):
            signal(barrier, {"expert": peer("expert", by), "section": peer("section", hop)})
    for axis in ("groups", "shard", "section"):
        for by in range(1, sizes[axis]):
            signal(barrier, {axis: peer(axis, by)})
    greeted = sum(n - 1 for n in sizes.values()) + (experts - 1) * (sections - 1)

    def token_copy(m):
        return pltpu.make_async_copy(tokens.at[m], held.at[m], tok_sem.at[m])

    for m in range(micro):
        token_copy(m).start()
    own = [
        pltpu.make_async_copy(sources[a], weights.at[a, me_s], own_sem.at[a]) for a in range(3)
    ]
    for copy in own:
        copy.start()

    meta_own = pltpu.make_async_copy(meta_here, meta_v.at[me_s], meta_own_sem)

    def hand_back(m):
        return remote(
            held.at[m], out.at[m], hand_sem.at[0, m], hand_sem.at[1, m],
            {"section": peer("section", sections - 1)},
        )

    def comb_copy():
        return remote(
            comb, comb_in, comb_sem.at[0], comb_sem.at[1], {"section": peer("section", 1)}
        )

    def part(group, a, k, shard):
        return weights.at[a, shard, pl.ds(group * half + k * step, step)]

    def over_shard(a, k, by):
        i = k * 3 + a
        src = sources[a].at[pl.ds(me_g * half + k * step, step)]
        return remote(
            src, part(me_g, a, k, me_s), wx_send.at[i, by], wx_recv.at[i, by],
            {"shard": peer("shard", by)},
        )

    def over_groups(a, k, by, hop):
        i = k * 3 + a
        spot = part(me_g, a, k, peer("shard", shards - by))
        return remote(
            spot, spot, wy_send.at[i, by, hop], wy_recv.at[i, by, hop],
            {"groups": peer("groups", hop)},
        )

    def meta_over_shard(by):
        return remote(
            meta_here, meta_v.at[me_s], meta_send_sem.at[by], meta_recv_sem.at[by],
            {"shard": peer("shard", by)},
        )

    order = [(a, k, by) for k in range(cuts) for a in range(3) for by in range(1, shards)]

    def start_weights():
        for a, k, by in order:
            over_shard(a, k, by).start()

    def relay_weights(begin, end):
        for a, k, by in order:
            if begin <= k < end:
                over_shard(a, k, by).wait_recv()
                for hop in range(1, groups):
                    over_groups(a, k, by, hop).start()

    def finish_relay(at):
        for a, k, by in order:
            if k == at:
                for hop in range(1, groups):
                    over_groups(a, k, by, hop).wait()

    def partner(by):
        if experts & (experts - 1):
            return peer("expert", by)
        other, bit = me_e, 1
        while bit < experts:
            if by & bit:
                other = other + bit * (1 - 2 * lax.rem(me_e // bit, 2))
            bit *= 2
        return other

    def source(by):
        if experts & (experts - 1):
            return peer("expert", experts - by)
        return partner(by)

    far_first = sorted(range(1, experts), key=lambda by: (by < experts // 2, by))

    def chunk_out(m, by):
        return remote(
            send.at[m, partner(by)], recv[m].at[me_e], disp_send.at[m, by],
            disp_recv.at[m, by], {"expert": partner(by)},
        )

    def chunk_self(m):
        return pltpu.make_async_copy(send.at[m, me_e], recv[m].at[me_e], disp_self.at[m])

    def back_on(m, by):
        where = {"section": peer("section", 1)}
        if by > 0:
            where["expert"] = partner(by)
        return remote(
            ret_send.at[m, partner(by)], ret_recv.at[0, m, me_e], back_send.at[0, m, by],
            back_recv.at[0, m, by], where,
        )

    def back_home(m, by):
        return remote(
            ret_send.at[m, partner(by)], ret_recv.at[1, m, me_e], back_send.at[1, m, by],
            back_recv.at[1, m, by], {"expert": partner(by)},
        )

    def back_own(m):
        return pltpu.make_async_copy(
            ret_send.at[m, me_e], ret_recv.at[1, m, me_e], back_self.at[m]
        )

    def lanes(r):
        return pl.ds(pl.multiple_of(r * blk, blk), blk)

    def tail_line(e, j):
        return pl.ds(e * tail + j, blocks, stride=tails_all)

    def tail_part(j):
        return pl.ds(blocks + j * folds, folds)

    def put(dst, r, values):
        for e in range(experts):
            dst(e)[r] = values[e * main:(e + 1) * main].astype(BF16)
        tails_by[r] = values[experts * main:]

    def spread_tails(dst, e):
        for j in range(tail):
            lines = tails[tail_line(e, j), :].astype(BF16)
            dst(e)[tail_part(j)] = lines.reshape(folds, main, blk)

    def collect_tails(src):
        for e in range(experts):
            for j in range(tail):
                lines = src(e)[tail_part(j)].reshape(blocks, blk)
                tails[tail_line(e, j), :] = lines.astype(F32)

    def take(src, r):
        pieces_of = [src(e)[r] for e in range(experts)]
        return jnp.concatenate(pieces_of + [tails_by[r].astype(BF16)], axis=0)

    def dispatch(m):
        values = held[m].astype(F32)
        scale = lax.rsqrt(jnp.mean(values * values, axis=-1, keepdims=True) + EPS)
        normed[...] = (values * scale * gain[...]).astype(BF16)

        @pl.loop(0, blocks, unroll=8)
        def _(r):
            put(
                lambda e: send.at[m, e], r,
                jnp.dot(disp[m], normed[:, lanes(r)], preferred_element_type=F32),
            )

        for e in range(experts):
            spread_tails(lambda e: send.at[m, e], e)

    def send_chunks(m):
        for by in far_first:
            chunk_out(m, by).start()
        chunk_self(m).start()

    def segment(m, s, k):
        products = []
        for group in range(groups):
            for u in range(step):
                c = group * half + k * step + u
                at = (k * groups + group) * step + u
                x = take(lambda e: recv[m].at[e], meta_s[s, 0, c])
                gate = jnp.dot(x, weights[0, s, c], preferred_element_type=F32)
                up = jnp.dot(x, weights[1, s, c], preferred_element_type=F32)
                hidden = (gate / (1.0 + jnp.exp(-gate)) * up).astype(BF16)
                product = jnp.dot(hidden, weights[2, s, c], preferred_element_type=F32)
                products.append((at, c, product))
        for at, c, product in products:
            parts[s, at] = product + parts[s, meta_s[s, 1, c]]

    def expert_part(m, opening):
        chunk_self(m).wait()
        for by in far_first:
            chunk_out(m, by).wait()
        collect_tails(lambda e: recv[m].at[e])
        if opening:
            for copy in own:
                copy.wait()
            for by in range(1, shards):
                meta_over_shard(by).wait()
            meta_own.wait()
            load = pltpu.make_async_copy(meta_v, meta_s, meta_copy_sem)
            load.start()
            load.wait()
            for k in range(cuts):
                segment(m, me_s, k)
            for k in range(cuts):
                if early + k < cuts:
                    @pl.when(first)
                    def _():
                        relay_weights(early + k, early + k + 1)
                if early + k == cuts - 1:
                    @pl.when(first & (me_l < sections - 1))
                    def _():
                        signal(go_sem, {"section": peer("section", 1)})
                finish_relay(k)

                @pl.loop(1, shards)
                def _(by):
                    segment(m, peer("shard", shards - by), k)
            for a, k, by in order:
                over_shard(a, k, by).wait_send()
        else:
            @pl.loop(0, shards)
            def _(s):
                for k in range(cuts):
                    segment(m, s, k)

        @pl.loop(0, blocks, unroll=4)
        def _(j):
            total = parts[0, meta_s[0, 2, j]]
            for s in range(1, shards):
                total = total + parts[s, meta_s[s, 2, j]]
            put(lambda e: ret_send.at[m, e], j, total)

        for e in range(experts):
            spread_tails(lambda e: ret_send.at[m, e], e)

        @pl.when(me_l < sections - 1)
        def _():
            for by in far_first + [0]:
                back_on(m, by).start()

        @pl.when(last)
        def _():
            for by in far_first:
                back_home(m, by).start()
            back_own(m).start()

    def combine(m, which, dst):
        collect_tails(lambda e: ret_recv.at[which, m, e])

        @pl.loop(0, blocks, unroll=8)
        def _(r):
            mixed = jnp.dot(
                pieces[which, m], take(lambda e: ret_recv.at[which, m, e], r),
                preferred_element_type=F32,
            )
            mixed = mixed[:rows] + mixed[rows:2 * rows] + mixed[2 * rows:]
            dst[m, :, lanes(r)] = (held[m, :, lanes(r)].astype(F32) + mixed).astype(BF16)

    def split(which, m, value):
        for i in range(3):
            piece = value.astype(BF16)
            pieces[which, m, i * rows:(i + 1) * rows, :] = piece
            value = value - piece.astype(F32)

    def arrival(c):
        group = sum((c >= g * half).astype(jnp.int32) for g in range(1, groups))
        within = c - group * half
        k = sum((within >= i * step).astype(jnp.int32) for i in range(1, cuts))
        return k * (groups - 1) * step + group * step + within

    def iota(shape, axis):
        return lax.broadcasted_iota(jnp.int32, shape, axis)

    slot = iota((slots, rows), 0)
    inner = slot - experts * main
    head = inner < 0
    expert_main = sum((slot >= e * main).astype(jnp.int32) for e in range(1, experts))
    expert_tail = sum((inner >= e * tail).astype(jnp.int32) for e in range(1, experts + 1))
    expert = jnp.where(head, expert_main, expert_tail)
    place_in = jnp.where(head, slot - expert_main * main, main + inner - expert_tail * tail)
    place_in = place_in.astype(F32)
    earlier = (iota((rows, rows), 0) < iota((rows, rows), 1)).astype(F32).astype(BF16)
    for m in range(micro):
        named = [ids[m, j:j + 1, :] == expert for j in range(TOP)]
        hit = functools.reduce(jnp.logical_or, named)
        ahead = jnp.dot(
            hit.astype(F32).astype(BF16), earlier, preferred_element_type=F32
        )
        fits = hit & (ahead == place_in)
        amount = sum(jnp.where(named[j], mix[m, j:j + 1, :], 0.0) for j in range(TOP))
        disp[m] = fits.astype(F32).astype(BF16)
        comb[m] = jnp.transpose(jnp.where(fits, amount, 0.0))

    cols = cols_in[...]
    cols_down = jnp.transpose(jnp.broadcast_to(cols, (n_blk, n_blk)))
    from_place = arrival(iota((n_blk, n_blk), 0))
    chained = (cols_down == cols) & (from_place < arrival(iota((n_blk, n_blk), 1)))
    before = jnp.max(jnp.where(chained, from_place, -1), axis=0, keepdims=True)
    final = jnp.broadcast_to(cols_down[:, :1], (n_blk, blocks)) == iota((n_blk, blocks), 1)
    last_at = jnp.where(final, arrival(iota((n_blk, blocks), 0)), -1)
    last_at = jnp.max(last_at, axis=0, keepdims=True)
    meta_here[...] = jnp.zeros_like(meta_here)
    meta_here[0:1, 0:n_blk] = rows_in[...]
    meta_here[1:2, 0:n_blk] = jnp.where(before < 0, n_blk, before)
    meta_here[2:3, 0:blocks] = jnp.where(last_at < 0, n_blk, last_at)
    for s in range(shards):
        parts[s, n_blk] = jnp.zeros_like(parts[s, n_blk])
    early = cuts * 5 // 8

    for m in range(micro):
        token_copy(m).wait()

    @pl.when(first)
    def _():
        dispatch(0)

    @pl.when(last)
    def _():
        for m in range(micro):
            split(1, m, comb[m])

    pl.semaphore_wait(barrier, greeted)

    for by in range(1, shards):
        meta_over_shard(by).start()
    meta_own.start()

    @pl.when(first)
    def _():
        send_chunks(0)
        start_weights()

    @pl.when(me_l < sections - 1)
    def _():
        comb_copy().start()

    @pl.when(first)
    def _():
        for m in range(1, micro):
            dispatch(m)
            send_chunks(m)
        relay_weights(0, early)

    @pl.when(me_l > 0)
    def _():
        comb_copy().wait_recv()
        for m in range(micro):
            split(0, m, comb_in[m])
        pl.semaphore_wait(go_sem, 1)
        start_weights()
        for m in range(micro):
            if m == 0:
                relay_weights(0, cuts if micro == 1 else cuts - 1)
            if m == 1:
                relay_weights(cuts - 1, cuts)
            for by in far_first + [0]:
                back_on(m, by).wait_recv()
            combine(m, 0, held)
            hand_back(m).start()
            dispatch(m)
            send_chunks(m)

    for m in range(micro):
        expert_part(m, m == 0)

    @pl.when(last)
    def _():
        for m in range(micro):
            back_own(m).wait()
            for by in far_first:
                back_home(m, by).wait()
            combine(m, 1, out)

    @pl.when(me_l > 0)
    def _():
        for m in range(micro):
            hand_back(m).wait_send()

    @pl.when(me_l < sections - 1)
    def _():
        comb_copy().wait_send()
        for m in range(micro):
            for by in far_first + [0]:
                back_on(m, by).wait_send()
            hand_back(m).wait_recv()


def body(
    sizes,
    tokens,
    norm_gain,
    route_ids,
    route_weights,
    gate_blocks,
    up_blocks,
    down_blocks,
    gate_rows,
    down_cols,
):
    groups, shards, experts, sections = sizes
    assert sections == 2
    micro, rows, width = tokens.shape
    n_blk, blk = gate_blocks.shape[2], gate_blocks.shape[-1]
    blocks = width // blk
    cap = min(rows, max(rows * 9 // 16, rows * TOP // experts + 2))
    main = cap // 16 * 16
    tails_all = -(-(experts * (cap - main)) // 8) * 8
    slots = experts * main + tails_all

    cuts = math.gcd(n_blk // groups, CUTS)
    meta_width = -(-max(n_blk, blocks) // 128) * 128
    pieces = 3 * cuts
    dims = (micro, rows, blocks, blk, cap, experts, shards, groups, sections, n_blk)
    dma = pltpu.SemaphoreType.DMA
    assert blocks % main == 0
    chunk = (micro, experts, cap * blocks // main, main, blk)
    vmem, anywhere = pl.BlockSpec(memory_space=pltpu.VMEM), pl.BlockSpec(memory_space=pltpu.HBM)
    out = pl.pallas_call(
        functools.partial(layer_kernel, dims),
        out_shape=pltpu.VMEM((micro, rows, width), BF16),
        in_specs=[anywhere] + [vmem] * 3 + [anywhere] * 3 + [vmem] * 2,
        out_specs=vmem,
        scratch_shapes=[
            pltpu.VMEM((micro, rows, width), BF16),
            pltpu.VMEM((micro, slots, rows), BF16),
            pltpu.VMEM((micro, rows, slots), F32),
            pltpu.VMEM((micro, rows, slots), F32),
            pltpu.VMEM((2, micro, 3 * rows, slots), BF16),
            pltpu.VMEM((8, meta_width), jnp.int32),
            pltpu.VMEM((rows, width), BF16),
            pltpu.VMEM((tails_all * blocks, blk), F32),
            pltpu.VMEM(chunk, BF16),
            [pltpu.VMEM(chunk[1:], BF16) for _ in range(micro)],
            pltpu.VMEM((shards, n_blk + 1, slots, blk), F32),
            pltpu.VMEM(chunk, BF16),
            pltpu.VMEM((2,) + chunk, BF16),
            pltpu.VMEM((3, shards, n_blk, blk, blk), BF16),
            pltpu.VMEM((shards, 8, meta_width), jnp.int32),
            pltpu.SMEM((shards, 8, meta_width), jnp.int32),
            dma((micro,)),
            dma((2, micro)),
            dma((3,)),
            dma,
            dma((shards,)),
            dma((shards,)),
            dma,
            dma((2,)),
            dma((pieces, shards)),
            dma((pieces, shards)),
            dma((pieces, shards, groups)),
            dma((pieces, shards, groups)),
            dma((micro, experts)),
            dma((micro, experts)),
            dma((micro,)),
            dma((2, micro, experts)),
            dma((2, micro, experts)),
            dma((micro,)),
            pltpu.SemaphoreType.REGULAR,
        ],
        compiler_params=pltpu.CompilerParams(
            collective_id=0, has_side_effects=True, vmem_limit_bytes=56 * 1024 * 1024
        ),
    )(
        tokens, norm_gain, jnp.swapaxes(route_ids[0], 1, 2), jnp.swapaxes(route_weights[0], 1, 2),
        gate_blocks.reshape(n_blk, blk, blk), up_blocks.reshape(n_blk, blk, blk),
        down_blocks.reshape(n_blk, blk, blk), gate_rows.reshape(1, n_blk),
        down_cols.reshape(1, n_blk),
    )
    return out[None]


def solution(mesh):
    sizes = tuple(mesh.shape[name] for name in ("groups", "shard", "expert", "section"))
    in_specs = (
        P(None, ("groups", "shard", "expert"), None),
        P("section", None),
        P("section", None, ("groups", "shard", "expert"), None),
        P("section", None, ("groups", "shard", "expert"), None),
        P("section", "expert", "shard", None, None, None),
        P("section", "expert", "shard", None, None, None),
        P("section", "expert", "shard", None, None, None),
        P("section", "expert", "shard", None),
        P("section", "expert", "shard", None),
    )
    out_specs = P("section", None, ("groups", "shard", "expert"), None)
    return jax.shard_map(
        functools.partial(body, sizes), mesh=mesh, in_specs=in_specs, out_specs=out_specs,
        check_vma=False,
    )
```

time: 96.3 us -> 103 us (1.070)
  the two profiles are of different devices: /device:TPU:9 before, /device:TPU:11 now
where the time goes in v1:
time: 103 us
  Pallas kernels  102 us (99%)
    pallas_call x1, Pallas kernels, body(): pl.pallas_call(functools.partial(layer_kernel, dims), out_shape=pltpu.VME...  102 us

profile of v1, /device:TPU:11, one launch (start us, length us, event | category | flops | bytes accessed | tf_op | source)
XLA Modules:
  0.0 102.9 jit_solution(7946577737431151050)
XLA Ops:
  0.0 102.0 %shard_map.91 = bf16[2,32,6144]{2,1,0:T(8,128)(2,1)S(1)} custom-call(bf16[2,32,6144]{2,1,0:T(8,128)(2,1)} %tokens.1, f32[1,6144]{1,0:T(1,128)} %gain.1, s32[2,2,32]{2,1,0:T(2,128)} %bitcast.16, f32[2,2,32]{2,1,0:T(2,128)} %bitcast.17, bf16[32,128,128]{2,1,0:T(8,128)(2,1)} %bitcast.13, bf16[32,128,128]{2,1,0:T(8,128)(2,1)} %bitcast.14, ...), custom_call_target="tpu_custom_call" | custom-call | tf_op jit(solution)/shard_map/pallas_call | solution.py:475
  102.0 0.9 copy.11

commit v2 on v1

--- a/solution.py
+++ b/solution.py
@@ -12,7 +12,15 @@
 EPS = 1e-05
 BF16 = jnp.bfloat16
 F32 = jnp.float32
-CUTS = 8
+
+
+def cut_list(half):
+    cuts, at = [], 0
+    while at < half:
+        size = min(4, max(1, (half - at) // 2))
+        cuts.append((at, size))
+        at += size
+    return cuts
 
 
 def layer_kernel(
@@ -20,10 +28,10 @@
     tokens, gain, ids, mix, gate_hbm, up_hbm, down_hbm, rows_in, cols_in,
     out,
     held, disp, comb, comb_in, pieces, meta_here, normed, tails, send, recv, parts, ret_send, ret_recv,
-    weights, meta_v, meta_s,
+    weights, stage, meta_v, meta_s,
     tok_sem, hand_sem, own_sem, meta_own_sem, meta_send_sem, meta_recv_sem, meta_copy_sem, comb_sem,
     wx_send, wx_recv, wy_send, wy_recv, disp_send, disp_recv, disp_self,
-    back_send, back_recv, back_self, go_sem,
+    back_send, back_recv, back_self, sx_send, sx_recv, sc_send, sc_recv, sy_send, sy_recv,
 ):
     micro, rows, blocks, blk, cap, experts, shards, groups, sections, n_blk = dims
     main = cap // 16 * 16
@@ -37,8 +45,7 @@
     sizes = {"groups": groups, "shard": shards, "expert": experts, "section": sections}
     place = {"groups": me_g, "shard": me_s, "expert": me_e, "section": me_l}
     half = n_blk // groups
-    cuts = math.gcd(half, CUTS)
-    step = half // cuts
+    cuts = cut_list(half)
     sources = (gate_hbm, up_hbm, down_hbm)
     first, last = me_l == 0, me_l == sections - 1
 
@@ -55,25 +62,21 @@
         pl.semaphore_signal(sem, inc=1, device_id=device, device_id_type=pl.DeviceIdType.MESH)
 
     barrier = pltpu.get_barrier_semaphore()
-    for by in range(experts - 1, 0, -1):
-        signal(barrier, {"expert": peer("expert", by)})
-        for hop in range(1, sections):
-            signal(barrier, {"expert": peer("expert", by), "section": peer("section", hop)})
-    for axis in ("groups", "shard", "section"):
-        for by in range(1, sizes[axis]):
-            signal(barrier, {axis: peer(axis, by)})
-    greeted = sum(n - 1 for n in sizes.values()) + (experts - 1) * (sections - 1)
+    for axis in ("expert", "shard", "groups"):
+        for by in range(sizes[axis] - 1, 0, -1):
+            for hop in range(sections):
+                signal(barrier, {axis: peer(axis, by), "section": peer("section", hop)})
+    for hop in range(1, sections):
+        signal(barrier, {"section": peer("section", hop)})
+    greeted = sections * (groups + shards + experts - 2) - 1
 
     def token_copy(m):
         return pltpu.make_async_copy(tokens.at[m], held.at[m], tok_sem.at[m])
 
     for m in range(micro):
         token_copy(m).start()
-    own = [
-        pltpu.make_async_copy(sources[a], weights.at[a, me_s], own_sem.at[a]) for a in range(3)
-    ]
-    for copy in own:
-        copy.start()
+    for a in range(3):
+        pltpu.make_async_copy(sources[a], weights.at[a, me_s], own_sem).start()
 
     meta_own = pltpu.make_async_copy(meta_here, meta_v.at[me_s], meta_own_sem)
 
@@ -88,89 +91,137 @@
             comb, comb_in, comb_sem.at[0], comb_sem.at[1], {"section": peer("section", 1)}
         )
 
-    def part(group, a, k, shard):
-        return weights.at[a, shard, pl.ds(group * half + k * step, step)]
-
-    def over_shard(a, k, by):
-        i = k * 3 + a
-        src = sources[a].at[pl.ds(me_g * half + k * step, step)]
-        return remote(
-            src, part(me_g, a, k, me_s), wx_send.at[i, by], wx_recv.at[i, by],
+    def spot(group, k, shard):
+        return weights.at[:, shard, pl.ds(group * half + cuts[k][0], cuts[k][1])]
+
+    def staged(k, shard):
+        return stage.at[:, shard, pl.ds(*cuts[k])]
+
+    def origin(by):
+        return peer("shard", shards - by)
+
+    def own_part(a, k):
+        return sources[a].at[pl.ds(me_g * half + cuts[k][0], cuts[k][1])]
+
+    pairs = [(k, by) for k in range(len(cuts)) for by in range(1, shards)]
+    others = stage.at[:, pl.ds(0, shards - 1)]
+
+    def start_stage():
+        for k, by in pairs:
+            for a in range(3):
+                remote(
+                    own_part(a, k), stage.at[a, me_s, pl.ds(*cuts[k])], sx_send,
+                    sx_recv.at[k, by - 1],
+                    {"shard": peer("shard", by), "section": peer("section", 1)},
+                ).start()
+
+    def stage_in(k, by):
+        at = staged(k, origin(by))
+        return remote(at, at, sx_send, sx_recv.at[k, by - 1], {"section": peer("section", 1)})
+
+    def stage_down(k, by):
+        return remote(
+            staged(k, origin(by)), spot(me_g, k, origin(by)), sc_send, sc_recv.at[k, by - 1],
+            {"section": peer("section", 1)},
+        )
+
+    def stage_over(k, by, hop, from_g):
+        return remote(
+            staged(k, origin(by)), spot(from_g, k, origin(by)), sy_send.at[hop - 1],
+            sy_recv.at[k, by - 1, hop - 1],
+            {"groups": peer("groups", hop), "section": peer("section", 1)},
+        )
+
+    def start_weights():
+        for k, by in pairs:
+            for a in range(3):
+                remote(
+                    own_part(a, k),
+                    weights.at[a, me_s, pl.ds(me_g * half + cuts[k][0], cuts[k][1])],
+                    wx_send, wx_recv.at[k, by - 1], {"shard": peer("shard", by)},
+                ).start()
+
+    def weights_in(k, by):
+        at = spot(me_g, k, origin(by))
+        return remote(at, at, wx_send, wx_recv.at[k, by - 1], {"shard": peer("shard", by)})
+
+    def weights_over(k, by, hop, from_g):
+        at = spot(from_g, k, origin(by))
+        return remote(
+            at, at, wy_send.at[hop - 1], wy_recv.at[k, by - 1, hop - 1],
+            {"groups": peer("groups", hop)},
+        )
+
+    def all_sent(sem):
+        remote(others, others, sem, wx_recv.at[0, 0], {"shard": peer("shard", 1)}).wait_send()
+
+    def meta_over_shard(by):
+        return remote(
+            meta_here, meta_v.at[me_s], meta_send_sem.at[by - 1], meta_recv_sem.at[by - 1],
             {"shard": peer("shard", by)},
         )
 
-    def over_groups(a, k, by, hop):
-        i = k * 3 + a
-        spot = part(me_g, a, k, peer("shard", shards - by))
-        return remote(
-            spot, spot, wy_send.at[i, by, hop], wy_recv.at[i, by, hop],
-            {"groups": peer("groups", hop)},
-        )
-
-    def meta_over_shard(by):
-        return remote(
-            meta_here, meta_v.at[me_s], meta_send_sem.at[by], meta_recv_sem.at[by],
-            {"shard": peer("shard", by)},
-        )
-
-    order = [(a, k, by) for k in range(cuts) for a in range(3) for by in range(1, shards)]
-
-    def start_weights():
-        for a, k, by in order:
-            over_shard(a, k, by).start()
-
     def relay_weights(begin, end):
-        for a, k, by in order:
+        for k, by in pairs:
             if begin <= k < end:
-                over_shard(a, k, by).wait_recv()
+                weights_in(k, by).wait_recv()
                 for hop in range(1, groups):
-                    over_groups(a, k, by, hop).start()
+                    weights_over(k, by, hop, me_g).start()
 
     def finish_relay(at):
-        for a, k, by in order:
+        for k, by in pairs:
             if k == at:
                 for hop in range(1, groups):
-                    over_groups(a, k, by, hop).wait()
-
-    def partner(by):
-        if experts & (experts - 1):
-            return peer("expert", by)
-        other, bit = me_e, 1
-        while bit < experts:
-            if by & bit:
-                other = other + bit * (1 - 2 * lax.rem(me_e // bit, 2))
-            bit *= 2
-        return other
-
-    def source(by):
-        if experts & (experts - 1):
-            return peer("expert", experts - by)
-        return partner(by)
-
-    far_first = sorted(range(1, experts), key=lambda by: (by < experts // 2, by))
+                    weights_over(k, by, hop, peer("groups", groups - hop)).wait_recv()
+
+    def finish_stage(at):
+        for k, by in pairs:
+            if k == at:
+                stage_down(k, by).wait_recv()
+                for hop in range(1, groups):
+                    stage_over(k, by, hop, peer("groups", groups - hop)).wait_recv()
+
+    far_first = sorted(range(1, experts), key=lambda by: abs(by - experts // 2))
 
     def chunk_out(m, by):
-        return remote(
-            send.at[m, partner(by)], recv[m].at[me_e], disp_send.at[m, by],
-            disp_recv.at[m, by], {"expert": partner(by)},
+        e = peer("expert", by)
+        return remote(
+            send.at[m, e], recv[m].at[me_e], disp_send.at[m], disp_recv.at[m], {"expert": e}
         )
 
     def chunk_self(m):
         return pltpu.make_async_copy(send.at[m, me_e], recv[m].at[me_e], disp_self.at[m])
 
+    def chunks_far(m):
+        return remote(
+            send.at[m, pl.ds(0, experts - 1)], recv[m].at[pl.ds(0, experts - 1)],
+            disp_send.at[m], disp_recv.at[m], {"expert": peer("expert", 1)},
+        )
+
     def back_on(m, by):
-        where = {"section": peer("section", 1)}
-        if by > 0:
-            where["expert"] = partner(by)
-        return remote(
-            ret_send.at[m, partner(by)], ret_recv.at[0, m, me_e], back_send.at[0, m, by],
-            back_recv.at[0, m, by], where,
+        e = peer("expert", by)
+        return remote(
+            ret_send.at[m, e], ret_recv.at[0, m, me_e], back_send.at[m], back_recv.at[0, m],
+            {"expert": e, "section": peer("section", 1)},
+        )
+
+    def back_on_all(m):
+        return remote(
+            ret_send.at[m], ret_recv.at[0, m], back_send.at[m], back_recv.at[0, m],
+            {"section": peer("section", 1)},
         )
 
     def back_home(m, by):
-        return remote(
-            ret_send.at[m, partner(by)], ret_recv.at[1, m, me_e], back_send.at[1, m, by],
-            back_recv.at[1, m, by], {"expert": partner(by)},
+        e = peer("expert", by)
+        return remote(
+            ret_send.at[m, e], ret_recv.at[1, m, me_e], back_send.at[m], back_recv.at[1, m],
+            {"expert": e},
+        )
+
+    def back_far(m):
+        return remote(
+            ret_send.at[m, pl.ds(0, experts - 1)], ret_recv.at[1, m, pl.ds(0, experts - 1)],
+            back_send.at[m], back_recv.at[1, m], {"expert": peer("expert", 1)},
         )
 
     def back_own(m):
@@ -229,10 +280,11 @@
 
     def segment(m, s, k):
         products = []
+        start, size = cuts[k]
         for group in range(groups):
-            for u in range(step):
-                c = group * half + k * step + u
-                at = (k * groups + group) * step + u
+            for u in range(size):
+                c = group * half + start + u
+                at = groups * start + group * size + u
                 x = take(lambda e: recv[m].at[e], meta_s[s, 0, c])
                 gate = jnp.dot(x, weights[0, s, c], preferred_element_type=F32)
                 up = jnp.dot(x, weights[1, s, c], preferred_element_type=F32)
@@ -244,40 +296,35 @@
 
     def expert_part(m, opening):
         chunk_self(m).wait()
-        for by in far_first:
-            chunk_out(m, by).wait()
+        chunks_far(m).wait()
         collect_tails(lambda e: recv[m].at[e])
         if opening:
-            for copy in own:
-                copy.wait()
+            mine = weights.at[:, me_s]
+            pltpu.make_async_copy(mine, mine, own_sem).wait()
             for by in range(1, shards):
                 meta_over_shard(by).wait()
             meta_own.wait()
             load = pltpu.make_async_copy(meta_v, meta_s, meta_copy_sem)
             load.start()
             load.wait()
-            for k in range(cuts):
+            for k in range(len(cuts)):
                 segment(m, me_s, k)
-            for k in range(cuts):
-                if early + k < cuts:
-                    @pl.when(first)
-                    def _():
-                        relay_weights(early + k, early + k + 1)
-                if early + k == cuts - 1:
-                    @pl.when(first & (me_l < sections - 1))
-                    def _():
-                        signal(go_sem, {"section": peer("section", 1)})
-                finish_relay(k)
+            for k in range(len(cuts)):
+                @pl.when(first)
+                def _():
+                    finish_stage(k)
+
+                @pl.when(me_l > 0)
+                def _():
+                    finish_relay(k)
 
                 @pl.loop(1, shards)
                 def _(by):
                     segment(m, peer("shard", shards - by), k)
-            for a, k, by in order:
-                over_shard(a, k, by).wait_send()
         else:
             @pl.loop(0, shards)
             def _(s):
-                for k in range(cuts):
+                for k in range(len(cuts)):
                     segment(m, s, k)
 
         @pl.loop(0, blocks, unroll=4)
@@ -322,8 +369,14 @@
     def arrival(c):
         group = sum((c >= g * half).astype(jnp.int32) for g in range(1, groups))
         within = c - group * half
-        k = sum((within >= i * step).astype(jnp.int32) for i in range(1, cuts))
-        return k * (groups - 1) * step + group * step + within
+        start = sum(
+            (within >= cuts[k][0]).astype(jnp.int32) * cuts[k - 1][1] for k in range(1, len(cuts))
+        )
+        size = cuts[0][1] + sum(
+            (within >= cuts[k][0]).astype(jnp.int32) * (cuts[k][1] - cuts[k - 1][1])
+            for k in range(1, len(cuts))
+        )
+        return (groups - 1) * start + group * size + within
 
     def iota(shape, axis):
         return lax.broadcasted_iota(jnp.int32, shape, axis)
@@ -362,7 +415,6 @@
     meta_here[2:3, 0:blocks] = jnp.where(last_at < 0, n_blk, last_at)
     for s in range(shards):
         parts[s, n_blk] = jnp.zeros_like(parts[s, n_blk])
-    early = cuts * 5 // 8
 
     for m in range(micro):
         token_copy(m).wait()
@@ -384,8 +436,8 @@
 
     @pl.when(first)
     def _():
+        start_stage()
         send_chunks(0)
-        start_weights()
 
     @pl.when(me_l < sections - 1)
     def _():
@@ -396,22 +448,24 @@
         for m in range(1, micro):
             dispatch(m)
             send_chunks(m)
-        relay_weights(0, early)
 
     @pl.when(me_l > 0)
     def _():
+        for k, by in pairs:
+            stage_in(k, by).wait_recv()
+            for hop in range(1, groups):
+                stage_over(k, by, hop, me_g).start()
+            stage_down(k, by).start()
+        start_weights()
         comb_copy().wait_recv()
         for m in range(micro):
             split(0, m, comb_in[m])
-        pl.semaphore_wait(go_sem, 1)
-        start_weights()
         for m in range(micro):
             if m == 0:
-                relay_weights(0, cuts if micro == 1 else cuts - 1)
+                relay_weights(0, len(cuts) if micro == 1 else len(cuts) - 1)
             if m == 1:
-                relay_weights(cuts - 1, cuts)
-            for by in far_first + [0]:
-                back_on(m, by).wait_recv()
+                relay_weights(len(cuts) - 1, len(cuts))
+            back_on_all(m).wait_recv()
             combine(m, 0, held)
             hand_back(m).start()
             dispatch(m)
@@ -424,21 +478,25 @@
     def _():
         for m in range(micro):
             back_own(m).wait()
-            for by in far_first:
-                back_home(m, by).wait()
+            back_far(m).wait()
             combine(m, 1, out)
 
     @pl.when(me_l > 0)
     def _():
         for m in range(micro):
             hand_back(m).wait_send()
+        all_sent(wx_send)
+        all_sent(sc_send)
+        for hop in range(1, groups):
+            all_sent(sy_send.at[hop - 1])
+            all_sent(wy_send.at[hop - 1])
 
     @pl.when(me_l < sections - 1)
     def _():
         comb_copy().wait_send()
+        all_sent(sx_send)
         for m in range(micro):
-            for by in far_first + [0]:
-                back_on(m, by).wait_send()
+            back_on_all(m).wait_send()
             hand_back(m).wait_recv()
 
 
@@ -464,9 +522,8 @@
     tails_all = -(-(experts * (cap - main)) // 8) * 8
     slots = experts * main + tails_all
 
-    cuts = math.gcd(n_blk // groups, CUTS)
+    cuts = len(cut_list(n_blk // groups))
     meta_width = -(-max(n_blk, blocks) // 128) * 128
-    pieces = 3 * cuts
     dims = (micro, rows, blocks, blk, cap, experts, shards, groups, sections, n_blk)
     dma = pltpu.SemaphoreType.DMA
     assert blocks % main == 0
@@ -492,27 +549,33 @@
             pltpu.VMEM(chunk, BF16),
             pltpu.VMEM((2,) + chunk, BF16),
             pltpu.VMEM((3, shards, n_blk, blk, blk), BF16),
+            pltpu.VMEM((3, shards, n_blk // groups, blk, blk), BF16),
             pltpu.VMEM((shards, 8, meta_width), jnp.int32),
             pltpu.SMEM((shards, 8, meta_width), jnp.int32),
             dma((micro,)),
             dma((2, micro)),
-            dma((3,)),
             dma,
-            dma((shards,)),
-            dma((shards,)),
+            dma,
+            dma((shards - 1,)),
+            dma((shards - 1,)),
             dma,
             dma((2,)),
-            dma((pieces, shards)),
-            dma((pieces, shards)),
-            dma((pieces, shards, groups)),
-            dma((pieces, shards, groups)),
-            dma((micro, experts)),
-            dma((micro, experts)),
+            dma,
+            dma((cuts, shards - 1)),
+            dma((groups - 1,)),
+            dma((cuts, shards - 1, groups - 1)),
             dma((micro,)),
-            dma((2, micro, experts)),
-            dma((2, micro, experts)),
             dma((micro,)),
-            pltpu.SemaphoreType.REGULAR,
+            dma((micro,)),
+            dma((micro,)),
+            dma((2, micro)),
+            dma((micro,)),
+            dma,
+            dma((cuts, shards - 1)),
+            dma,
+            dma((cuts, shards - 1)),
+            dma((groups - 1,)),
+            dma((cuts, shards - 1, groups - 1)),
         ],
         compiler_params=pltpu.CompilerParams(
             collective_id=0, has_side_effects=True, vmem_limit_bytes=56 * 1024 * 1024

time: 103 us -> 97 us (0.942)
  the two profiles are of different devices: /device:TPU:11 before, /device:TPU:9 now
where the time goes in v2:
time: 97 us; the launch traced here: 96.2 us
  Pallas kernels  95.3 us (98%)
    pallas_call x1, Pallas kernels, body(): pl.pallas_call(functools.partial(layer_kernel, dims), out_shape=pltpu.VME...  95.3 us

profile of v2, /device:TPU:9, one launch (start us, length us, event | category | flops | bytes accessed | tf_op | source)
XLA Modules:
  0.0 96.2 jit_solution(11026888991995323785)
XLA Ops:
  0.0 95.3 %shard_map.91 = bf16[2,32,6144]{2,1,0:T(8,128)(2,1)S(1)} custom-call(bf16[2,32,6144]{2,1,0:T(8,128)(2,1)} %tokens.1, f32[1,6144]{1,0:T(1,128)} %gain.1, s32[2,2,32]{2,1,0:T(2,128)} %bitcast.16, f32[2,2,32]{2,1,0:T(2,128)} %bitcast.17, bf16[32,128,128]{2,1,0:T(8,128)(2,1)} %bitcast.13, bf16[32,128,128]{2,1,0:T(8,128)(2,1)} %bitcast.14, ...), custom_call_target="tpu_custom_call" | custom-call | tf_op jit(solution)/shard_map/pallas_call | solution.py:532
  95.3 0.9 copy.11

commit v3 on v2

--- a/solution.py
+++ b/solution.py
@@ -12,12 +12,14 @@
 EPS = 1e-05
 BF16 = jnp.bfloat16
 F32 = jnp.float32
+MOST = 2
+RUN = 4
 
 
 def cut_list(half):
     cuts, at = [], 0
     while at < half:
-        size = min(4, max(1, (half - at) // 2))
+        size = min(MOST, at + 1, (half - at + 1) // 2)
         cuts.append((at, size))
         at += size
     return cuts
@@ -278,19 +280,28 @@
             chunk_out(m, by).start()
         chunk_self(m).start()
 
-    def segment(m, s, k):
+    def listed(k):
+        start, size = cuts[k]
+        return [
+            (group * half + start + u, groups * start + group * size + u)
+            for group in range(groups) for u in range(size)
+        ]
+
+    whole = [item for k in range(len(cuts)) for item in listed(k)]
+
+    def segments(m, s, items):
+        for i in range(0, len(items), RUN):
+            segment(m, s, items[i:i + RUN])
+
+    def segment(m, s, items):
         products = []
-        start, size = cuts[k]
-        for group in range(groups):
-            for u in range(size):
-                c = group * half + start + u
-                at = groups * start + group * size + u
-                x = take(lambda e: recv[m].at[e], meta_s[s, 0, c])
-                gate = jnp.dot(x, weights[0, s, c], preferred_element_type=F32)
-                up = jnp.dot(x, weights[1, s, c], preferred_element_type=F32)
-                hidden = (gate / (1.0 + jnp.exp(-gate)) * up).astype(BF16)
-                product = jnp.dot(hidden, weights[2, s, c], preferred_element_type=F32)
-                products.append((at, c, product))
+        for c, at in items:
+            x = take(lambda e: recv[m].at[e], meta_s[s, 0, c])
+            gate = jnp.dot(x, weights[0, s, c], preferred_element_type=F32)
+            up = jnp.dot(x, weights[1, s, c], preferred_element_type=F32)
+            hidden = (gate / (1.0 + jnp.exp(-gate)) * up).astype(BF16)
+            product = jnp.dot(hidden, weights[2, s, c], preferred_element_type=F32)
+            products.append((at, c, product))
         for at, c, product in products:
             parts[s, at] = product + parts[s, meta_s[s, 1, c]]
 
@@ -307,8 +318,7 @@
             load = pltpu.make_async_copy(meta_v, meta_s, meta_copy_sem)
             load.start()
             load.wait()
-            for k in range(len(cuts)):
-                segment(m, me_s, k)
+            segments(m, me_s, whole)
             for k in range(len(cuts)):
                 @pl.when(first)
                 def _():
@@ -320,12 +330,11 @@
 
                 @pl.loop(1, shards)
                 def _(by):
-                    segment(m, peer("shard", shards - by), k)
+                    segments(m, peer("shard", shards - by), listed(k))
         else:
             @pl.loop(0, shards)
             def _(s):
-                for k in range(len(cuts)):
-                    segment(m, s, k)
+                segments(m, s, whole)
 
         @pl.loop(0, blocks, unroll=4)
         def _(j):

time: 97 us -> 95.5 us (0.985)
  Pallas kernels: 95.3 us -> 93.8 us
    pallas_call x1, Pallas kernels: 95.3 us -> 93.8 us  [body(): pl.pallas_call(functools.partial(layer_kernel, dims), out_shape=pltpu.VME...]
where the time goes in v3:
time: 95.5 us; the launch traced here: 94.7 us
  Pallas kernels  93.8 us (98%)
    pallas_call x1, Pallas kernels, body(): pl.pallas_call(functools.partial(layer_kernel, dims), out_shape=pltpu.VME...  93.8 us

profile of v3, /device:TPU:9, one launch (start us, length us, event | category | flops | bytes accessed | tf_op | source)
XLA Modules:
  0.0 94.7 jit_solution(703490092212301439)
XLA Ops:
  0.0 93.8 %shard_map.91 = bf16[2,32,6144]{2,1,0:T(8,128)(2,1)S(1)} custom-call(bf16[2,32,6144]{2,1,0:T(8,128)(2,1)} %tokens.1, f32[1,6144]{1,0:T(1,128)} %gain.1, s32[2,2,32]{2,1,0:T(2,128)} %bitcast.16, f32[2,2,32]{2,1,0:T(2,128)} %bitcast.17, bf16[32,128,128]{2,1,0:T(8,128)(2,1)} %bitcast.13, bf16[32,128,128]{2,1,0:T(8,128)(2,1)} %bitcast.14, ...), custom_call_target="tpu_custom_call" | custom-call | tf_op jit(solution)/shard_map/pallas_call | solution.py:541
  93.8 0.9 copy.11

commit v4 on v3

--- a/solution.py
+++ b/solution.py
@@ -16,10 +16,14 @@
 RUN = 4
 
 
-def cut_list(half):
+def both_ways(half, groups):
+    return half // 16 if groups > 1 else 0
+
+
+def cut_list(keep):
     cuts, at = [], 0
-    while at < half:
-        size = min(MOST, at + 1, (half - at + 1) // 2)
+    while at < keep:
+        size = min(MOST, at + 1, (keep - at + 1) // 2)
         cuts.append((at, size))
         at += size
     return cuts
@@ -47,8 +51,11 @@
     sizes = {"groups": groups, "shard": shards, "expert": experts, "section": sections}
     place = {"groups": me_g, "shard": me_s, "expert": me_e, "section": me_l}
     half = n_blk // groups
-    cuts = cut_list(half)
+    extra = both_ways(half, groups)
+    keep = half - extra
+    cuts = cut_list(keep)
     sources = (gate_hbm, up_hbm, down_hbm)
+    pieces_in = len(cuts) + min(extra, 1)
     first, last = me_l == 0, me_l == sections - 1
 
     def remote(src, dst, ssem, rsem, device):
@@ -97,23 +104,27 @@
         return weights.at[:, shard, pl.ds(group * half + cuts[k][0], cuts[k][1])]
 
     def staged(k, shard):
+        if k == len(cuts):
+            return stage.at[:, shard, pl.ds(keep, groups * extra)]
         return stage.at[:, shard, pl.ds(*cuts[k])]
 
     def origin(by):
         return peer("shard", shards - by)
 
-    def own_part(a, k):
-        return sources[a].at[pl.ds(me_g * half + cuts[k][0], cuts[k][1])]
-
-    pairs = [(k, by) for k in range(len(cuts)) for by in range(1, shards)]
-    others = stage.at[:, pl.ds(0, shards - 1)]
+    def outgoing(k):
+        if k == len(cuts):
+            return [(q * half + keep, keep + q * extra, extra) for q in range(groups)]
+        return [(me_g * half + cuts[k][0], cuts[k][0], cuts[k][1])]
+
+    relayed = [(k, by) for k in range(len(cuts)) for by in range(1, shards)]
+    pairs = [(k, by) for k in range(pieces_in) for by in range(1, shards)]
 
     def start_stage():
         for k, by in pairs:
-            for a in range(3):
+            for c, to, size in outgoing(k):
                 remote(
-                    own_part(a, k), stage.at[a, me_s, pl.ds(*cuts[k])], sx_send,
-                    sx_recv.at[k, by - 1],
+                    weights.at[:, me_s, pl.ds(c, size)], stage.at[:, me_s, pl.ds(to, size)],
+                    sx_send, sx_recv.at[k, by - 1],
                     {"shard": peer("shard", by), "section": peer("section", 1)},
                 ).start()
 
@@ -121,11 +132,17 @@
         at = staged(k, origin(by))
         return remote(at, at, sx_send, sx_recv.at[k, by - 1], {"section": peer("section", 1)})
 
+    def start_down(k, by):
+        for c, to, size in outgoing(k):
+            remote(
+                stage.at[:, origin(by), pl.ds(to, size)],
+                weights.at[:, origin(by), pl.ds(c, size)], sc_send, sc_recv.at[k, by - 1],
+                {"section": peer("section", 1)},
+            ).start()
+
     def stage_down(k, by):
-        return remote(
-            staged(k, origin(by)), spot(me_g, k, origin(by)), sc_send, sc_recv.at[k, by - 1],
-            {"section": peer("section", 1)},
-        )
+        at = staged(k, origin(by))
+        return remote(at, at, sc_send, sc_recv.at[k, by - 1], {"section": peer("section", 1)})
 
     def stage_over(k, by, hop, from_g):
         return remote(
@@ -136,15 +153,14 @@
 
     def start_weights():
         for k, by in pairs:
-            for a in range(3):
+            for c, to, size in outgoing(k):
+                at = weights.at[:, me_s, pl.ds(c, size)]
                 remote(
-                    own_part(a, k),
-                    weights.at[a, me_s, pl.ds(me_g * half + cuts[k][0], cuts[k][1])],
-                    wx_send, wx_recv.at[k, by - 1], {"shard": peer("shard", by)},
+                    at, at, wx_send, wx_recv.at[k, by - 1], {"shard": peer("shard", by)}
                 ).start()
 
     def weights_in(k, by):
-        at = spot(me_g, k, origin(by))
+        at = staged(k, origin(by))
         return remote(at, at, wx_send, wx_recv.at[k, by - 1], {"shard": peer("shard", by)})
 
     def weights_over(k, by, hop, from_g):
@@ -154,8 +170,9 @@
             {"groups": peer("groups", hop)},
         )
 
-    def all_sent(sem):
-        remote(others, others, sem, wx_recv.at[0, 0], {"shard": peer("shard", 1)}).wait_send()
+    def all_sent(sem, size=None):
+        at = stage.at[:, pl.ds(0, shards - 1), pl.ds(0, size or keep + groups * extra)]
+        remote(at, at, sem, wx_recv.at[0, 0], {"shard": peer("shard", 1)}).wait_send()
 
     def meta_over_shard(by):
         return remote(
@@ -167,11 +184,12 @@
         for k, by in pairs:
             if begin <= k < end:
                 weights_in(k, by).wait_recv()
-                for hop in range(1, groups):
-                    weights_over(k, by, hop, me_g).start()
+                if k < len(cuts):
+                    for hop in range(1, groups):
+                        weights_over(k, by, hop, me_g).start()
 
     def finish_relay(at):
-        for k, by in pairs:
+        for k, by in relayed:
             if k == at:
                 for hop in range(1, groups):
                     weights_over(k, by, hop, peer("groups", groups - hop)).wait_recv()
@@ -180,8 +198,9 @@
         for k, by in pairs:
             if k == at:
                 stage_down(k, by).wait_recv()
-                for hop in range(1, groups):
-                    stage_over(k, by, hop, peer("groups", groups - hop)).wait_recv()
+                if k < len(cuts):
+                    for hop in range(1, groups):
+                        stage_over(k, by, hop, peer("groups", groups - hop)).wait_recv()
 
     far_first = sorted(range(1, experts), key=lambda by: abs(by - experts // 2))
 
@@ -281,13 +300,18 @@
         chunk_self(m).start()
 
     def listed(k):
+        if k == len(cuts):
+            return [
+                (group * half + keep + u, groups * keep + group * extra + u)
+                for group in range(groups) for u in range(extra)
+            ]
         start, size = cuts[k]
         return [
             (group * half + start + u, groups * start + group * size + u)
             for group in range(groups) for u in range(size)
         ]
 
-    whole = [item for k in range(len(cuts)) for item in listed(k)]
+    whole = [item for k in range(pieces_in) for item in listed(k)]
 
     def segments(m, s, items):
         for i in range(0, len(items), RUN):
@@ -310,8 +334,6 @@
         chunks_far(m).wait()
         collect_tails(lambda e: recv[m].at[e])
         if opening:
-            mine = weights.at[:, me_s]
-            pltpu.make_async_copy(mine, mine, own_sem).wait()
             for by in range(1, shards):
                 meta_over_shard(by).wait()
             meta_own.wait()
@@ -319,7 +341,7 @@
             load.start()
             load.wait()
             segments(m, me_s, whole)
-            for k in range(len(cuts)):
+            for k in range(pieces_in):
                 @pl.when(first)
                 def _():
                     finish_stage(k)
@@ -385,7 +407,8 @@
             (within >= cuts[k][0]).astype(jnp.int32) * (cuts[k][1] - cuts[k - 1][1])
             for k in range(1, len(cuts))
         )
-        return (groups - 1) * start + group * size + within
+        early = (groups - 1) * start + group * size + within
+        return jnp.where(within < keep, early, groups * keep + group * extra + within - keep)
 
     def iota(shape, axis):
         return lax.broadcasted_iota(jnp.int32, shape, axis)
@@ -437,6 +460,8 @@
         for m in range(micro):
             split(1, m, comb[m])
 
+    mine = weights.at[:, me_s]
+    pltpu.make_async_copy(mine, mine, own_sem).wait()
     pl.semaphore_wait(barrier, greeted)
 
     for by in range(1, shards):
@@ -462,23 +487,26 @@
     def _():
         for k, by in pairs:
             stage_in(k, by).wait_recv()
-            for hop in range(1, groups):
-                stage_over(k, by, hop, me_g).start()
-            stage_down(k, by).start()
+            if k < len(cuts):
+                for hop in range(1, groups):
+                    stage_over(k, by, hop, me_g).start()
+            start_down(k, by)
         start_weights()
         comb_copy().wait_recv()
         for m in range(micro):
             split(0, m, comb_in[m])
         for m in range(micro):
             if m == 0:
-                relay_weights(0, len(cuts) if micro == 1 else len(cuts) - 1)
+                relay_weights(0, pieces_in if micro == 1 else pieces_in - 2)
             if m == 1:
-                relay_weights(len(cuts) - 1, len(cuts))
+                relay_weights(max(0, pieces_in - 2), pieces_in)
             back_on_all(m).wait_recv()
+            if m > 0:
+                send_chunks(m - 1)
             combine(m, 0, held)
             hand_back(m).start()
             dispatch(m)
-            send_chunks(m)
+        send_chunks(micro - 1)
 
     for m in range(micro):
         expert_part(m, m == 0)
@@ -497,8 +525,8 @@
         all_sent(wx_send)
         all_sent(sc_send)
         for hop in range(1, groups):
-            all_sent(sy_send.at[hop - 1])
-            all_sent(wy_send.at[hop - 1])
+            all_sent(sy_send.at[hop - 1], keep)
+            all_sent(wy_send.at[hop - 1], keep)
 
     @pl.when(me_l < sections - 1)
     def _():
@@ -531,7 +559,9 @@
     tails_all = -(-(experts * (cap - main)) // 8) * 8
     slots = experts * main + tails_all
 
-    cuts = len(cut_list(n_blk // groups))
+    extra = both_ways(n_blk // groups, groups)
+    keep = n_blk // groups - extra
+    cuts = len(cut_list(keep)) + min(extra, 1)
     meta_width = -(-max(n_blk, blocks) // 128) * 128
     dims = (micro, rows, blocks, blk, cap, experts, shards, groups, sections, n_blk)
     dma = pltpu.SemaphoreType.DMA
@@ -558,7 +588,7 @@
             pltpu.VMEM(chunk, BF16),
             pltpu.VMEM((2,) + chunk, BF16),
             pltpu.VMEM((3, shards, n_blk, blk, blk), BF16),
-            pltpu.VMEM((3, shards, n_blk // groups, blk, blk), BF16),
+            pltpu.VMEM((3, shards, keep + groups * extra, blk, blk), BF16),
             pltpu.VMEM((shards, 8, meta_width), jnp.int32),
             pltpu.SMEM((shards, 8, meta_width), jnp.int32),
             dma((micro,)),

time: 95.5 us -> 93.9 us (0.983)
  Pallas kernels: 93.8 us -> 92.8 us
    pallas_call x1, Pallas kernels: 93.8 us -> 92.8 us  [body(): pl.pallas_call(functools.partial(layer_kernel, dims), out_shape=pltpu.VME...]
where the time goes in v4:
time: 93.9 us; the launch traced here: 93.7 us
  Pallas kernels  92.8 us (99%)
    pallas_call x1, Pallas kernels, body(): pl.pallas_call(functools.partial(layer_kernel, dims), out_shape=pltpu.VME...  92.8 us

profile of v4, /device:TPU:9, one launch (start us, length us, event | category | flops | bytes accessed | tf_op | source)
XLA Modules:
  0.0 93.7 jit_solution(9598738225612056265)
XLA Ops:
  0.0 92.8 %shard_map.91 = bf16[2,32,6144]{2,1,0:T(8,128)(2,1)S(1)} custom-call(bf16[2,32,6144]{2,1,0:T(8,128)(2,1)} %tokens.1, f32[1,6144]{1,0:T(1,128)} %gain.1, s32[2,2,32]{2,1,0:T(2,128)} %bitcast.16, f32[2,2,32]{2,1,0:T(2,128)} %bitcast.17, bf16[32,128,128]{2,1,0:T(8,128)(2,1)} %bitcast.13, bf16[32,128,128]{2,1,0:T(8,128)(2,1)} %bitcast.14, ...), custom_call_target="tpu_custom_call" | custom-call | tf_op jit(solution)/shard_map/pallas_call | solution.py:571
  92.8 0.9 copy.11

commit v5 on v4

--- a/solution.py
+++ b/solution.py
@@ -202,7 +202,7 @@
                     for hop in range(1, groups):
                         stage_over(k, by, hop, peer("groups", groups - hop)).wait_recv()
 
-    far_first = sorted(range(1, experts), key=lambda by: abs(by - experts // 2))
+    far_first = sorted(range(1, experts), key=lambda by: (abs(by - experts // 2), -by))
 
     def chunk_out(m, by):
         e = peer("expert", by)

time: 93.9 us -> 92 us (0.980)
  Pallas kernels: 92.8 us -> 90.9 us
    pallas_call x1, Pallas kernels: 92.8 us -> 90.9 us  [body(): pl.pallas_call(functools.partial(layer_kernel, dims), out_shape=pltpu.VME...]
where the time goes in v5:
time: 92 us; the launch traced here: 91.8 us
  Pallas kernels  90.9 us (99%)
    pallas_call x1, Pallas kernels, body(): pl.pallas_call(functools.partial(layer_kernel, dims), out_shape=pltpu.VME...  90.9 us

profile of v5, /device:TPU:9, one launch (start us, length us, event | category | flops | bytes accessed | tf_op | source)
XLA Modules:
  0.0 91.8 jit_solution(2857334329993053299)
XLA Ops:
  0.0 90.9 %shard_map.91 = bf16[2,32,6144]{2,1,0:T(8,128)(2,1)S(1)} custom-call(bf16[2,32,6144]{2,1,0:T(8,128)(2,1)} %tokens.1, f32[1,6144]{1,0:T(1,128)} %gain.1, s32[2,2,32]{2,1,0:T(2,128)} %bitcast.16, f32[2,2,32]{2,1,0:T(2,128)} %bitcast.17, bf16[32,128,128]{2,1,0:T(8,128)(2,1)} %bitcast.13, bf16[32,128,128]{2,1,0:T(8,128)(2,1)} %bitcast.14, ...), custom_call_target="tpu_custom_call" | custom-call | tf_op jit(solution)/shard_map/pallas_call | solution.py:571
  90.9 0.9 copy.11

commit v6 on v5

--- a/solution.py
+++ b/solution.py
@@ -13,11 +13,11 @@
 BF16 = jnp.bfloat16
 F32 = jnp.float32
 MOST = 2
-RUN = 4
+RUN = 8
 
 
 def both_ways(half, groups):
-    return half // 16 if groups > 1 else 0
+    return half // 8 if groups > 1 else 0
 
 
 def cut_list(keep):
@@ -37,7 +37,7 @@
     weights, stage, meta_v, meta_s,
     tok_sem, hand_sem, own_sem, meta_own_sem, meta_send_sem, meta_recv_sem, meta_copy_sem, comb_sem,
     wx_send, wx_recv, wy_send, wy_recv, disp_send, disp_recv, disp_self,
-    back_send, back_recv, back_self, sx_send, sx_recv, sc_send, sc_recv, sy_send, sy_recv,
+    back_send, back_recv, back_self, sx_send, sx_recv, sc_send, sy_send,
 ):
     micro, rows, blocks, blk, cap, experts, shards, groups, sections, n_blk = dims
     main = cap // 16 * 16
@@ -136,18 +136,18 @@
         for c, to, size in outgoing(k):
             remote(
                 stage.at[:, origin(by), pl.ds(to, size)],
-                weights.at[:, origin(by), pl.ds(c, size)], sc_send, sc_recv.at[k, by - 1],
+                weights.at[:, origin(by), pl.ds(c, size)], sc_send, wx_recv.at[k, by - 1],
                 {"section": peer("section", 1)},
             ).start()
 
     def stage_down(k, by):
         at = staged(k, origin(by))
-        return remote(at, at, sc_send, sc_recv.at[k, by - 1], {"section": peer("section", 1)})
+        return remote(at, at, sc_send, wx_recv.at[k, by - 1], {"section": peer("section", 1)})
 
     def stage_over(k, by, hop, from_g):
         return remote(
             staged(k, origin(by)), spot(from_g, k, origin(by)), sy_send.at[hop - 1],
-            sy_recv.at[k, by - 1, hop - 1],
+            wy_recv.at[k, by - 1, hop - 1],
             {"groups": peer("groups", hop), "section": peer("section", 1)},
         )
 
@@ -250,8 +250,10 @@
             ret_send.at[m, me_e], ret_recv.at[1, m, me_e], back_self.at[m]
         )
 
-    def lanes(r):
-        return pl.ds(pl.multiple_of(r * blk, blk), blk)
+    wide = 2 - blocks % 2
+
+    def lanes(i):
+        return pl.ds(pl.multiple_of(i * wide * blk, wide * blk), wide * blk)
 
     def tail_line(e, j):
         return pl.ds(e * tail + j, blocks, stride=tails_all)
@@ -284,12 +286,11 @@
         scale = lax.rsqrt(jnp.mean(values * values, axis=-1, keepdims=True) + EPS)
         normed[...] = (values * scale * gain[...]).astype(BF16)
 
-        @pl.loop(0, blocks, unroll=8)
-        def _(r):
-            put(
-                lambda e: send.at[m, e], r,
-                jnp.dot(disp[m], normed[:, lanes(r)], preferred_element_type=F32),
-            )
+        @pl.loop(0, blocks // wide, unroll=True)
+        def _(i):
+            values = jnp.dot(disp[m], normed[:, lanes(i)], preferred_element_type=F32)
+            for j in range(wide):
+                put(lambda e: send.at[m, e], i * wide + j, values[:, j * blk:(j + 1) * blk])
 
         for e in range(experts):
             spread_tails(lambda e: send.at[m, e], e)
@@ -321,8 +322,9 @@
         products = []
         for c, at in items:
             x = take(lambda e: recv[m].at[e], meta_s[s, 0, c])
-            gate = jnp.dot(x, weights[0, s, c], preferred_element_type=F32)
-            up = jnp.dot(x, weights[1, s, c], preferred_element_type=F32)
+            both = jnp.concatenate([weights[0, s, c], weights[1, s, c]], axis=1)
+            both = jnp.dot(x, both, preferred_element_type=F32)
+            gate, up = both[:, :blk], both[:, blk:]
             hidden = (gate / (1.0 + jnp.exp(-gate)) * up).astype(BF16)
             product = jnp.dot(hidden, weights[2, s, c], preferred_element_type=F32)
             products.append((at, c, product))
@@ -358,7 +360,7 @@
             def _(s):
                 segments(m, s, whole)
 
-        @pl.loop(0, blocks, unroll=4)
+        @pl.loop(0, blocks, unroll=True)
         def _(j):
             total = parts[0, meta_s[0, 2, j]]
             for s in range(1, shards):
@@ -382,14 +384,15 @@
     def combine(m, which, dst):
         collect_tails(lambda e: ret_recv.at[which, m, e])
 
-        @pl.loop(0, blocks, unroll=8)
-        def _(r):
-            mixed = jnp.dot(
-                pieces[which, m], take(lambda e: ret_recv.at[which, m, e], r),
-                preferred_element_type=F32,
+        @pl.loop(0, blocks // wide, unroll=True)
+        def _(i):
+            values = jnp.concatenate(
+                [take(lambda e: ret_recv.at[which, m, e], i * wide + j) for j in range(wide)],
+                axis=1,
             )
+            mixed = jnp.dot(pieces[which, m], values, preferred_element_type=F32)
             mixed = mixed[:rows] + mixed[rows:2 * rows] + mixed[2 * rows:]
-            dst[m, :, lanes(r)] = (held[m, :, lanes(r)].astype(F32) + mixed).astype(BF16)
+            dst[m, :, lanes(i)] = (held[m, :, lanes(i)].astype(F32) + mixed).astype(BF16)
 
     def split(which, m, value):
         for i in range(3):
@@ -612,9 +615,7 @@
             dma,
             dma((cuts, shards - 1)),
             dma,
-            dma((cuts, shards - 1)),
             dma((groups - 1,)),
-            dma((cuts, shards - 1, groups - 1)),
         ],
         compiler_params=pltpu.CompilerParams(
             collective_id=0, has_side_effects=True, vmem_limit_bytes=56 * 1024 * 1024

time: 92 us -> 89.3 us (0.971)
  Pallas kernels: 90.9 us -> 88.2 us
    pallas_call x1, Pallas kernels: 90.9 us -> 88.2 us  [body(): pl.pallas_call(functools.partial(layer_kernel, dims), out_shape=pltpu.VME...]
where the time goes in v6:
time: 89.3 us; the launch traced here: 89.1 us
  Pallas kernels  88.2 us (99%)
    pallas_call x1, Pallas kernels, body(): pl.pallas_call(functools.partial(layer_kernel, dims), out_shape=pltpu.VME...  88.2 us

profile of v6, /device:TPU:9, one launch (start us, length us, event | category | flops | bytes accessed | tf_op | source)
XLA Modules:
  0.0 89.1 jit_solution(15050989379540420194)
XLA Ops:
  0.0 88.2 %shard_map.91 = bf16[2,32,6144]{2,1,0:T(8,128)(2,1)S(1)} custom-call(bf16[2,32,6144]{2,1,0:T(8,128)(2,1)} %tokens.1, f32[1,6144]{1,0:T(1,128)} %gain.1, s32[2,2,32]{2,1,0:T(2,128)} %bitcast.16, f32[2,2,32]{2,1,0:T(2,128)} %bitcast.17, bf16[32,128,128]{2,1,0:T(8,128)(2,1)} %bitcast.13, bf16[32,128,128]{2,1,0:T(8,128)(2,1)} %bitcast.14, ...), custom_call_target="tpu_custom_call" | custom-call | tf_op jit(solution)/shard_map/pallas_call | solution.py:574
  88.2 0.9 copy.11

commit v7 on v6

--- a/solution.py
+++ b/solution.py
@@ -37,7 +37,7 @@
     weights, stage, meta_v, meta_s,
     tok_sem, hand_sem, own_sem, meta_own_sem, meta_send_sem, meta_recv_sem, meta_copy_sem, comb_sem,
     wx_send, wx_recv, wy_send, wy_recv, disp_send, disp_recv, disp_self,
-    back_send, back_recv, back_self, sx_send, sx_recv, sc_send, sy_send,
+    back_send, back_recv, back_self, sx_send, sx_recv, sc_send, sy_send, go_sem,
 ):
     micro, rows, blocks, blk, cap, experts, shards, groups, sections, n_blk = dims
     main = cap // 16 * 16
@@ -122,11 +122,16 @@
     def start_stage():
         for k, by in pairs:
             for c, to, size in outgoing(k):
-                remote(
-                    weights.at[:, me_s, pl.ds(c, size)], stage.at[:, me_s, pl.ds(to, size)],
-                    sx_send, sx_recv.at[k, by - 1],
-                    {"shard": peer("shard", by), "section": peer("section", 1)},
-                ).start()
+                at = weights.at[:, me_s, pl.ds(c, size)]
+                if k < len(cuts):
+                    remote(
+                        at, stage.at[:, me_s, pl.ds(to, size)], sx_send, sx_recv.at[k, by - 1],
+                        {"shard": peer("shard", by), "section": peer("section", 1)},
+                    ).start()
+                else:
+                    remote(
+                        at, at, sx_send, wx_recv.at[k, by - 1], {"shard": peer("shard", by)}
+                    ).start()
 
     def stage_in(k, by):
         at = staged(k, origin(by))
@@ -342,19 +347,26 @@
             load = pltpu.make_async_copy(meta_v, meta_s, meta_copy_sem)
             load.start()
             load.wait()
-            segments(m, me_s, whole)
-            for k in range(pieces_in):
-                @pl.when(first)
-                def _():
+            @pl.when(first)
+            def _():
+                segments(m, me_s, whole)
+                for k in range(pieces_in):
                     finish_stage(k)
-
-                @pl.when(me_l > 0)
-                def _():
+                    if k == pieces_in - 1:
+                        signal(go_sem, {"section": peer("section", 1)})
+
+                    @pl.loop(1, shards)
+                    def _(by):
+                        segments(m, peer("shard", shards - by), listed(k))
+
+            @pl.when(me_l > 0)
+            def _():
+                for k in range(pieces_in):
                     finish_relay(k)
 
-                @pl.loop(1, shards)
-                def _(by):
-                    segments(m, peer("shard", shards - by), listed(k))
+                @pl.loop(0, shards)
+                def _(s):
+                    segments(m, s, whole)
         else:
             @pl.loop(0, shards)
             def _(s):
@@ -488,21 +500,20 @@
 
     @pl.when(me_l > 0)
     def _():
-        for k, by in pairs:
+        for k, by in relayed:
             stage_in(k, by).wait_recv()
-            if k < len(cuts):
-                for hop in range(1, groups):
-                    stage_over(k, by, hop, me_g).start()
+            for hop in range(1, groups):
+                stage_over(k, by, hop, me_g).start()
             start_down(k, by)
-        start_weights()
         comb_copy().wait_recv()
         for m in range(micro):
             split(0, m, comb_in[m])
+        pl.semaphore_wait(go_sem, 1)
+        start_weights()
+        early = max(0, pieces_in - 4)
         for m in range(micro):
             if m == 0:
-                relay_weights(0, pieces_in if micro == 1 else pieces_in - 2)
-            if m == 1:
-                relay_weights(max(0, pieces_in - 2), pieces_in)
+                relay_weights(0, early)
             back_on_all(m).wait_recv()
             if m > 0:
                 send_chunks(m - 1)
@@ -510,6 +521,7 @@
             hand_back(m).start()
             dispatch(m)
         send_chunks(micro - 1)
+        relay_weights(early, pieces_in)
 
     for m in range(micro):
         expert_part(m, m == 0)
@@ -526,7 +538,7 @@
         for m in range(micro):
             hand_back(m).wait_send()
         all_sent(wx_send)
-        all_sent(sc_send)
+        all_sent(sc_send, keep)
         for hop in range(1, groups):
             all_sent(sy_send.at[hop - 1], keep)
             all_sent(wy_send.at[hop - 1], keep)
@@ -616,6 +628,7 @@
             dma((cuts, shards - 1)),
             dma,
             dma((groups - 1,)),
+            pltpu.SemaphoreType.REGULAR,
         ],
         compiler_params=pltpu.CompilerParams(
             collective_id=0, has_side_effects=True, vmem_limit_bytes=56 * 1024 * 1024

time: 89.3 us -> 88.6 us (level)
  no operation moved by 1% of the time
where the time goes in v7:
time: 88.6 us; the launch traced here: 88.4 us
  Pallas kernels  87.5 us (99%)
    pallas_call x1, Pallas kernels, body(): pl.pallas_call(functools.partial(layer_kernel, dims), out_shape=pltpu.VME...  87.5 us

profile of v7, /device:TPU:9, one launch (start us, length us, event | category | flops | bytes accessed | tf_op | source)
XLA Modules:
  0.0 88.4 jit_solution(4004570397844224063)
XLA Ops:
  0.0 87.5 %shard_map.91 = bf16[2,32,6144]{2,1,0:T(8,128)(2,1)S(1)} custom-call(bf16[2,32,6144]{2,1,0:T(8,128)(2,1)} %tokens.1, f32[1,6144]{1,0:T(1,128)} %gain.1, s32[2,2,32]{2,1,0:T(2,128)} %bitcast.16, f32[2,2,32]{2,1,0:T(2,128)} %bitcast.17, bf16[32,128,128]{2,1,0:T(8,128)(2,1)} %bitcast.13, bf16[32,128,128]{2,1,0:T(8,128)(2,1)} %bitcast.14, ...), custom_call_target="tpu_custom_call" | custom-call | tf_op jit(solution)/shard_map/pallas_call | solution.py:586
  87.6 0.9 copy.11

commit v8 on v7

--- a/solution.py
+++ b/solution.py
@@ -510,7 +510,7 @@
             split(0, m, comb_in[m])
         pl.semaphore_wait(go_sem, 1)
         start_weights()
-        early = max(0, pieces_in - 4)
+        early = max(0, pieces_in - 5)
         for m in range(micro):
             if m == 0:
                 relay_weights(0, early)

time: 88.6 us -> 88.6 us (level)
  no operation moved by 1% of the time
where the time goes in v8:
time: 88.6 us; the launch traced here: 88.4 us
  Pallas kernels  87.5 us (99%)
    pallas_call x1, Pallas kernels, body(): pl.pallas_call(functools.partial(layer_kernel, dims), out_shape=pltpu.VME...  87.5 us

profile of v8, /device:TPU:9, one launch (start us, length us, event | category | flops | bytes accessed | tf_op | source)
XLA Modules:
  0.0 88.4 jit_solution(6094823666451868969)
XLA Ops:
  0.0 87.5 %shard_map.91 = bf16[2,32,6144]{2,1,0:T(8,128)(2,1)S(1)} custom-call(bf16[2,32,6144]{2,1,0:T(8,128)(2,1)} %tokens.1, f32[1,6144]{1,0:T(1,128)} %gain.1, s32[2,2,32]{2,1,0:T(2,128)} %bitcast.16, f32[2,2,32]{2,1,0:T(2,128)} %bitcast.17, bf16[32,128,128]{2,1,0:T(8,128)(2,1)} %bitcast.13, bf16[32,128,128]{2,1,0:T(8,128)(2,1)} %bitcast.14, ...), custom_call_target="tpu_custom_call" | custom-call | tf_op jit(solution)/shard_map/pallas_call | solution.py:586
  87.6 0.9 copy.11
